TPU v7x, 128 devices: a whole 4x4x4 slice. The times are simulated.
128 devices in a mesh: member: 2 (over y_hi), gridy: 8 (over x, core), gridx: 8 (over z, y_lo).
Axes of the slice: x: 4, y: 4 (y_hi: 2, y_lo: 2; y = y_hi * 2 + y_lo), z: 4, core: 2. Of those that a mesh axis runs over, the one named last changes fastest.
Arguments:
- temp: float32 [4, 4, 512, 2048], P('member', None, 'gridy', 'gridx'), may hold values from -6 to 6
- salt: float32 [4, 4, 512, 2048], P('member', None, 'gridy', 'gridx'), may hold values from -6 to 6
- uvel: float32 [4, 4, 512, 2048], P('member', None, 'gridy', 'gridx'), may hold values from -3 to 3
- vvel: float32 [4, 4, 512, 2048], P('member', None, 'gridy', 'gridx'), may hold values from -3 to 3
- eta: float32 [4, 512, 2048], P('member', 'gridy', 'gridx'), may hold values from -6 to 6
- land_mask: int32 [512, 2048], P('gridy', 'gridx'), may hold values 0 or 1
- clone_source: int32 [4], P('member'), may hold values from 0 to 3
Outputs:
- new_temp: float32 [4, 4, 512, 2048], P('member', None, 'gridy', 'gridx')
- new_salt: float32 [4, 4, 512, 2048], P('member', None, 'gridy', 'gridx')
- new_uvel: float32 [4, 4, 512, 2048], P('member', None, 'gridy', 'gridx')
- new_vvel: float32 [4, 4, 512, 2048], P('member', None, 'gridy', 'gridx')
- new_eta: float32 [4, 512, 2048], P('member', 'gridy', 'gridx')
- overturning: float32 [4, 4, 512], P('member', None, 'gridy')
- clone_weight: float32 [4], P('member')
All inputs are finite; a program needn't handle non-finite values. No bound on the sum of `land_mask` on one device may be relied on, other than what follows from the above.
Results may differ from a plain program's by a relative error of at most 0.0001.
Values sent between devices are 32-bit elements; how exact they have to be, the bound alone decides.
A program may use at most 128 MiB of HBM per device.

v0:
```python
import jax
import jax.numpy as jnp
from jax import lax
from jax.sharding import PartitionSpec as P

STEPS = 2
ITERS = 3
ALPHA_T = 0.8
BETA_S = 0.6
PRESS_K = 0.25
STEP_DT = 0.1
KAPPA = 0.1
VISCOSITY = 0.1
DRAG_K = 0.05
CORI_K = 1.0
SURF_C = 4.0
DIV_K = 0.5
GRAV_K = 0.5


def padded_2(block, sides, width):
    for axis, dim in sides:
        count = lax.axis_size(axis)
        forward = [(i, i + 1) for i in range(count - 1)]
        forward.append((count - 1, 0))
        backward = [(target, source) for source, target in forward]
        low = lax.ppermute(
            lax.slice_in_dim(block, block.shape[dim] - width, None, axis=dim), axis, forward
        )
        high = lax.ppermute(lax.slice_in_dim(block, 0, width, axis=dim), axis, backward)
        block = jnp.concatenate([low, block, high], axis=dim)
    return block


def tree_sum(values, axes):
    for axis in axes:
        count = lax.axis_size(axis)
        step = 1
        while step < count:
            pairs = [(i, i ^ step) for i in range(count)]
            values = values + lax.ppermute(values, axis, pairs)
            step *= 2
    return values


def pressure(temp, salt):
    return PRESS_K * jnp.cumsum(BETA_S * salt - ALPHA_T * temp, axis=-3)


def split_rims(padded, south_keep, north_keep):
    east_side = padded[..., 1:-1, 2:]
    west_side = padded[..., 1:-1, :-2]
    north_side = padded[..., 2:, 1:-1]
    south_side = padded[..., :-2, 1:-1]
    north_side = north_side.at[..., -1, :].multiply(north_keep)
    south_side = south_side.at[..., 0, :].multiply(south_keep)
    return (east_side, west_side, north_side, south_side)


def volume_sides(fields, south_keep, north_keep):
    padded = padded_2(jnp.stack(fields), (("gridy", 3), ("gridx", 4)), 1)
    return split_rims(padded, south_keep, north_keep)


def surface_sides(fields, south_keep, north_keep):
    padded = padded_2(jnp.stack(fields), (("gridy", 2), ("gridx", 3)), 1)
    return split_rims(padded, south_keep, north_keep)


def surface_apply(field, south_keep, north_keep):
    east_side, west_side, north_side, south_side = surface_sides((field,), south_keep, north_keep)
    return (1.0 + 4.0 * SURF_C) * field - SURF_C * (
        east_side[0] + west_side[0] + north_side[0] + south_side[0]
    )


def member_total(values):
    return jnp.sum(values, axis=(1, 2))


def squared_norm(residual):
    return tree_sum(member_total(residual * residual), ("gridy", "gridx"))


def widen(values):
    return values[:, None, None]


def surface_solve(rhs, south_keep, north_keep):
    solution = jnp.zeros_like(rhs)
    residual = rhs
    direction = rhs
    norm_now = squared_norm(residual)
    for count in range(ITERS):
        image = surface_apply(direction, south_keep, north_keep)
        alpha = norm_now / tree_sum(member_total(direction * image), ("gridy", "gridx"))
        solution = solution + widen(alpha) * direction
        residual = residual - widen(alpha) * image
        norm_next = squared_norm(residual)
        direction = residual + widen(norm_next / norm_now) * direction
        norm_now = norm_next
    return solution


def shards(temp, salt, uvel, vvel, eta, land_mask, clone_source):
    levels = temp.shape[1]
    rows = temp.shape[2]
    cols = temp.shape[3]
    ocean = land_mask.astype(jnp.float32)
    tile_row = lax.axis_index("gridy")
    tile_count = lax.axis_size("gridy")
    total_rows = rows * tile_count
    total_cols = cols * lax.axis_size("gridx")
    south_keep = (tile_row > 0).astype(jnp.float32)
    north_keep = (tile_row < tile_count - 1).astype(jnp.float32)
    latitude = (tile_row * rows + jnp.arange(rows, dtype=jnp.int32)).astype(jnp.float32) + 0.5
    coriolis = (CORI_K * (2.0 * latitude / total_rows - 1.0))[:, None]
    for count in range(STEPS):
        press = pressure(temp, salt)
        east_side, west_side, north_side, south_side = volume_sides(
            (temp, salt, uvel, vvel, press), south_keep, north_keep
        )
        lap_temp = east_side[0] + west_side[0] + north_side[0] + south_side[0] - 4.0 * temp
        lap_salt = east_side[1] + west_side[1] + north_side[1] + south_side[1] - 4.0 * salt
        lap_uvel = east_side[2] + west_side[2] + north_side[2] + south_side[2] - 4.0 * uvel
        lap_vvel = east_side[3] + west_side[3] + north_side[3] + south_side[3] - 4.0 * vvel
        temp_next = ocean * (
            temp
            - STEP_DT
            * 0.5
            * (uvel * (east_side[0] - west_side[0]) + vvel * (north_side[0] - south_side[0]))
            + KAPPA * lap_temp
        )
        salt_next = ocean * (
            salt
            - STEP_DT
            * 0.5
            * (uvel * (east_side[1] - west_side[1]) + vvel * (north_side[1] - south_side[1]))
            + KAPPA * lap_salt
        )
        ustar = ocean * (
            uvel
            + STEP_DT * (coriolis * vvel - 0.5 * (east_side[4] - west_side[4]) - DRAG_K * uvel)
            + VISCOSITY * lap_uvel
        )
        vstar = ocean * (
            vvel
            + STEP_DT * (-coriolis * uvel - 0.5 * (north_side[4] - south_side[4]) - DRAG_K * vvel)
            + VISCOSITY * lap_vvel
        )
        trans_u = jnp.sum(ustar, axis=1)
        trans_v = jnp.sum(vstar, axis=1)
        east_t, west_t, north_t, south_t = surface_sides((trans_u, trans_v), south_keep, north_keep)
        rhs = eta - DIV_K * 0.5 * (east_t[0] - west_t[0] + (north_t[1] - south_t[1]))
        eta = surface_solve(rhs, south_keep, north_keep)
        east_e, west_e, north_e, south_e = surface_sides((eta,), south_keep, north_keep)
        uvel = ocean * (ustar - GRAV_K * 0.5 * (east_e[0] - west_e[0])[:, None])
        vvel = ocean * (vstar - GRAV_K * 0.5 * (north_e[0] - south_e[0])[:, None])
        temp = temp_next
        salt = salt_next
    zonal_scale = 1.0 / jnp.sqrt(jnp.float32(total_cols))
    score_scale = 1.0 / jnp.sqrt(jnp.float32(levels * total_rows))
    lat_weight = latitude / total_rows
    zonal_local = jnp.sum(vvel, axis=3)
    zonal_whole = tree_sum(zonal_local, ("gridx",))
    overturn = jnp.cumsum(zonal_whole, axis=1) * zonal_scale
    score = tree_sum(jnp.sum(overturn * lat_weight, axis=(1, 2)) * score_scale, ("gridy",))
    state_stack = jnp.stack((temp, salt, uvel, vvel))
    every_state, every_eta, every_score = (
        lax.all_gather(state_stack, "member", axis=1, tiled=True),
        lax.all_gather(eta, "member", axis=0, tiled=True),
        lax.all_gather(score, "member", axis=0, tiled=True),
    )
    picked = jnp.take(every_state, clone_source, axis=1)
    new_eta = jnp.take(every_eta, clone_source, axis=0)
    clone_weight = jnp.take(every_score, clone_source, axis=0) - jnp.mean(every_score)
    return (picked[0], picked[1], picked[2], picked[3], new_eta, overturn, clone_weight)


def solution(mesh):
    in_specs = (
        P("member", None, "gridy", "gridx"),
        P("member", None, "gridy", "gridx"),
        P("member", None, "gridy", "gridx"),
        P("member", None, "gridy", "gridx"),
        P("member", "gridy", "gridx"),
        P("gridy", "gridx"),
        P("member"),
    )
    out_specs = (
        P("member", None, "gridy", "gridx"),
        P("member", None, "gridy", "gridx"),
        P("member", None, "gridy", "gridx"),
        P("member", None, "gridy", "gridx"),
        P("member", "gridy", "gridx"),
        P("member", None, "gridy"),
        P("member"),
    )
    return jax.shard_map(shards, mesh=mesh, in_specs=in_specs, out_specs=out_specs, check_vma=False)
```

profile of v0, /device:TPU:1, one launch (start us, length us, event | category | flops | bytes accessed | tf_op | source)
XLA Modules:
  0.0 543.2 jit_solution(18020476195742906736)
XLA Ops:
  23.0 3.5 collective-permute-start.2
  43.5 4.2 collective-permute-start.5
  49.1 3.6 collective-permute-start.6
  57.2 3.4 collective-permute-start.15
  61.9 3.9 collective-permute-start.16
  67.9 4.2 collective-permute-start.18
  91.1 5.9 %collective-permute-start.24 = (f32[2]{0:T(128)S(1)}, f32[2]{0:T(128)S(1)}, u32[]{:S(2)}, u32[]{:S(2)}) collective-permute-start(f32[2]{0:T(128)S(1)} %get-tuple-element.322), channel_id=1, source_target_pairs={{0,8},{8,0},{16,24},{24,16},{32,40},{40,32},{48,56},{56,48},{1,9},... | collective-permute-start | bytes 32 | tf_op jit(solution)/shard_map/ppermute | solution.py:41
  113.0 6.0 %collective-permute-start.31 = (f32[1,2,1,256]{3,2,1,0:T(1,128)S(1)}, f32[1,2,1,256]{3,2,1,0:T(1,128)S(1)}, u32[]{:S(2)}, u32[]{:S(2)}) collective-permute-start(f32[1,2,1,256]{3,2,1,0:T(1,128)S(1)} %get-tuple-element.409), channel_id=1, source_target_pairs={{8,0},{16,8},{24,16},{32,24},{40,32},{48,40},{56,48},{0,56},{9,1},... | collective-permute-start | bytes 6152 | tf_op jit(solution)/shard_map/ppermute | solution.py:30
  125.9 4.2 collective-permute-start.34
  133.7 3.6 collective-permute-done.36
  146.1 6.1 %collective-permute-start.40 = (f32[2]{0:T(128)S(1)}, f32[2]{0:T(128)S(1)}, u32[]{:S(2)}, u32[]{:S(2)}) collective-permute-start(f32[2]{0:T(128)S(1)} %multiply_reduce_fusion.5), channel_id=1, source_target_pairs={{0,8},{8,0},{16,24},{24,16},{32,40},{40,32},{48,56},{56,48},{1,9},... | collective-permute-start | bytes 32 | tf_op jit(solution)/shard_map/ppermute | solution.py:41
  155.7 3.6 collective-permute-done.42
  168.6 6.1 %collective-permute-start.47 = (f32[1,2,1,256]{3,2,1,0:T(1,128)S(1)}, f32[1,2,1,256]{3,2,1,0:T(1,128)S(1)}, u32[]{:S(2)}, u32[]{:S(2)}) collective-permute-start(f32[1,2,1,256]{3,2,1,0:T(1,128)S(1)} %get-tuple-element.405), channel_id=1, source_target_pairs={{8,0},{16,8},{24,16},{32,24},{40,32},{48,40},{56,48},{0,56},{9,1},... | collective-permute-start | bytes 6152 | tf_op jit(solution)/shard_map/ppermute | solution.py:30
  174.7 3.6 bitcast_dynamic-update-slice_fusion.3
  207.4 5.7 %collective-permute-start.56 = (f32[1,2,1,256]{3,2,1,0:T(1,128)S(1)}, f32[1,2,1,256]{3,2,1,0:T(1,128)S(1)}, u32[]{:S(2)}, u32[]{:S(2)}) collective-permute-start(f32[1,2,1,256]{3,2,1,0:T(1,128)S(1)} %get-tuple-element.401), channel_id=1, source_target_pairs={{0,8},{8,16},{16,24},{24,32},{32,40},{40,48},{48,56},{56,0},{1,9},... | collective-permute-start | bytes 6152 | tf_op jit(solution)/shard_map/ppermute | solution.py:27
  213.5 3.5 bitcast_dynamic-update-slice_fusion.2
  217.2 3.6 collective-permute-start.58
  228.0 4.1 collective-permute-start.61
  240.9 3.9 collective-permute-start.62
  244.8 3.0 pad_maximum_fusion.3
  258.4 3.4 fusion.178
  264.9 3.7 collective-permute-start.65
  270.6 3.6 collective-permute-start.66
  279.2 3.7 collective-permute-start.75
  284.8 3.6 collective-permute-start.76
  294.3 3.8 collective-permute-start.78
  316.1 6.5 %collective-permute-start.84 = (f32[2]{0:T(128)S(1)}, f32[2]{0:T(128)S(1)}, u32[]{:S(2)}, u32[]{:S(2)}) collective-permute-start(f32[2]{0:T(128)S(1)} %get-tuple-element.307), channel_id=1, source_target_pairs={{0,8},{8,0},{16,24},{24,16},{32,40},{40,32},{48,56},{56,48},{1,9},... | collective-permute-start | bytes 32 | tf_op jit(solution)/shard_map/ppermute | solution.py:41
  339.0 6.1 %collective-permute-start.91 = (f32[1,2,1,256]{3,2,1,0:T(1,128)S(1)}, f32[1,2,1,256]{3,2,1,0:T(1,128)S(1)}, u32[]{:S(2)}, u32[]{:S(2)}) collective-permute-start(f32[1,2,1,256]{3,2,1,0:T(1,128)S(1)} %get-tuple-element.395), channel_id=1, source_target_pairs={{8,0},{16,8},{24,16},{32,24},{40,32},{48,40},{56,48},{0,56},{9,1},... | collective-permute-start | bytes 6152 | tf_op jit(solution)/shard_map/ppermute | solution.py:30
  356.6 3.4 collective-permute-start.94
  363.8 3.4 collective-permute-done.96
  372.5 3.4 collective-permute-done.99
  377.6 6.1 %collective-permute-start.100 = (f32[2]{0:T(128)S(1)}, f32[2]{0:T(128)S(1)}, u32[]{:S(2)}, u32[]{:S(2)}) collective-permute-start(f32[2]{0:T(128)S(1)} %multiply_reduce_fusion), channel_id=1, source_target_pairs={{0,8},{8,0},{16,24},{24,16},{32,40},{40,32},{48,56},{56,48},{1,9},... | collective-permute-start | bytes 32 | tf_op jit(solution)/shard_map/ppermute | solution.py:41
  387.4 3.4 collective-permute-done.102
  396.1 3.4 collective-permute-done.105
  401.6 6.1 %collective-permute-start.107 = (f32[1,2,1,256]{3,2,1,0:T(1,128)S(1)}, f32[1,2,1,256]{3,2,1,0:T(1,128)S(1)}, u32[]{:S(2)}, u32[]{:S(2)}) collective-permute-start(f32[1,2,1,256]{3,2,1,0:T(1,128)S(1)} %get-tuple-element.391), channel_id=1, source_target_pairs={{8,0},{16,8},{24,16},{32,24},{40,32},{48,40},{56,48},{0,56},{9,1},... | collective-permute-start | bytes 6152 | tf_op jit(solution)/shard_map/ppermute | solution.py:30
  409.6 3.6 collective-permute-start.108
  419.2 3.7 collective-permute-start.110
  426.1 3.9 collective-permute-done.112
  435.3 3.4 collective-permute-done.115
  440.4 6.1 %collective-permute-start.117 = (f32[1,2,1,256]{3,2,1,0:T(1,128)S(1)}, f32[1,2,1,256]{3,2,1,0:T(1,128)S(1)}, u32[]{:S(2)}, u32[]{:S(2)}) collective-permute-start(f32[1,2,1,256]{3,2,1,0:T(1,128)S(1)} %get-tuple-element.388), channel_id=1, source_target_pairs={{8,0},{16,8},{24,16},{32,24},{40,32},{48,40},{56,48},{0,56},{9,1},... | collective-permute-start | bytes 6152 | tf_op jit(solution)/shard_map/ppermute | solution.py:30
  447.8 3.6 collective-permute-start.118
  456.9 3.4 fusion.87
  472.0 6.0 %all_gather.10 = f32[4,64,256]{2,1,0:T(8,128)S(1)} all-gather(f32[2,64,256]{2,1,0:T(8,128)S(1)} %copy-done.28), channel_id=1, replica_groups=mesh['member'=2,'gridy'=8,'gridx'=8] {'member'}, dimensions={0}, use_global_device_ids=true | all-gather | bytes 393216 | tf_op jit(solution)/shard_map/all_gather | solution.py:171
  478.6 9.3 %collective-permute-start.123 = (f32[2]{0:T(128)S(1)}, f32[2]{0:T(128)S(1)}, u32[]{:S(2)}, u32[]{:S(2)}) collective-permute-start(f32[2]{0:T(128)S(1)} %broadcast_multiply_fusion.9), channel_id=1, source_target_pairs={{0,8},{8,0},{16,24},{24,16},{32,40},{40,32},{48,56},{56,48},{1,9},... | collective-permute-start | bytes 32 | tf_op jit(solution)/shard_map/ppermute | solution.py:41
  491.5 4.3 collective-permute-done.125
  496.5 5.8 %all-reduce = f32[4]{0:T(128)S(1)} all-reduce(f32[4]{0:T(128)S(1)} %add_dynamic-update-slice_fusion), channel_id=1, replica_groups=mesh['member'=2,'gridy'=8,'gridx'=8] {'member'}, use_global_device_ids=true, to_apply=%add | all-reduce | flops 4 | bytes 32
  505.4 23.3 %all-gather.2.cloned.1.call-done = f32[4,4,4,64,256]{4,3,2,1,0:T(8,128)} async-done(((f32[4,2,4,64,256]{4,3,2,1,0:T(8,128)}), f32[4,4,4,64,256]{4,3,2,1,0:T(8,128)}) %all-gather.2.cloned.1.call-update) | async-done | bytes 4194320 | tf_op jit(solution)/shard_map/all_gather | solution.py:170
  528.6 4.3 gather_fusion
  (552 shorter events, 297.3 us)
Async XLA Ops:
  7.2 521.5 %all-gather.2.cloned.1.call-start = ((), (), s32[]{:S(2)}) async-start(), calls=%async_computation | async-start | bytes 6291456 | tf_op jit(solution)/shard_map/all_gather | solution.py:170
  11.0 4.3 collective-permute-start.1
  19.8 14.3 %collective-permute-start.3 = (f32[5,2,4,66,1]{3,2,4,1,0:T(4,128)S(1)}, f32[5,2,4,66,1]{3,2,4,1,0:T(4,128)S(1)}, u32[]{:S(2)}, u32[]{:S(2)}) collective-permute-start(f32[5,2,4,66,1]{3,2,4,1,0:T(4,128)S(1)} %copy.16), channel_id=1, source_target_pairs={{0,1},{1,2},{2,3},{3,4},{4,5},{5,6},{6,7},{7,0},{8,9},{9,10},{10,1... | collective-permute-start | bytes 31688 | tf_op jit(solution)/shard_map/ppermute | solution.py:27
  23.0 12.7 %collective-permute-start.2 = (f32[5,2,4,66,1]{3,2,4,1,0:T(4,128)S(1)}, f32[5,2,4,66,1]{3,2,4,1,0:T(4,128)S(1)}, u32[]{:S(2)}, u32[]{:S(2)}) collective-permute-start(f32[5,2,4,66,1]{3,2,4,1,0:T(4,128)S(1)} %copy.14), channel_id=1, source_target_pairs={{1,0},{2,1},{3,2},{4,3},{5,4},{6,5},{7,6},{0,7},{9,8},{10,9},{11,1... | collective-permute-start | bytes 31688 | tf_op jit(solution)/shard_map/ppermute | solution.py:30
  43.5 5.0 collective-permute-start.5
  49.1 6.2 %collective-permute-start.7 = (f32[2,2,66,1]{3,2,1,0:T(8,128)S(1)}, f32[2,2,66,1]{3,2,1,0:T(8,128)S(1)}, u32[]{:S(2)}, u32[]{:S(2)}) collective-permute-start(f32[2,2,66,1]{3,2,1,0:T(8,128)S(1)} %get-tuple-element.356), channel_id=1, source_target_pairs={{0,1},{1,2},{2,3},{3,4},{4,5},{5,6},{6,7},{7,0},{8,9},{9,10},{10,1... | collective-permute-start | bytes 3176 | tf_op jit(solution)/shard_map/ppermute | solution.py:27
  49.1 6.9 %collective-permute-start.6 = (f32[2,2,66,1]{3,2,1,0:T(8,128)S(1)}, f32[2,2,66,1]{3,2,1,0:T(8,128)S(1)}, u32[]{:S(2)}, u32[]{:S(2)}) collective-permute-start(f32[2,2,66,1]{3,2,1,0:T(8,128)S(1)} %get-tuple-element.355), channel_id=1, source_target_pairs={{1,0},{2,1},{3,2},{4,3},{5,4},{6,5},{7,6},{0,7},{9,8},{10,9},{11,1... | collective-permute-start | bytes 3176 | tf_op jit(solution)/shard_map/ppermute | solution.py:30
  61.8 5.7 %collective-permute-start.17 = (f32[1,2,66,1]{3,2,1,0:T(8,128)S(1)}, f32[1,2,66,1]{3,2,1,0:T(8,128)S(1)}, u32[]{:S(2)}, u32[]{:S(2)}) collective-permute-start(f32[1,2,66,1]{3,2,1,0:T(8,128)S(1)} %get-tuple-element.380), channel_id=1, source_target_pairs={{0,1},{1,2},{2,3},{3,4},{4,5},{5,6},{6,7},{7,0},{8,9},{9,10},{10,1... | collective-permute-start | bytes 1592 | tf_op jit(solution)/shard_map/ppermute | solution.py:27
  61.9 5.7 %collective-permute-start.16 = (f32[1,2,66,1]{3,2,1,0:T(8,128)S(1)}, f32[1,2,66,1]{3,2,1,0:T(8,128)S(1)}, u32[]{:S(2)}, u32[]{:S(2)}) collective-permute-start(f32[1,2,66,1]{3,2,1,0:T(8,128)S(1)} %get-tuple-element.379), channel_id=1, source_target_pairs={{1,0},{2,1},{3,2},{4,3},{5,4},{6,5},{7,6},{0,7},{9,8},{10,9},{11,1... | collective-permute-start | bytes 1592 | tf_op jit(solution)/shard_map/ppermute | solution.py:30
  67.9 5.1 collective-permute-start.18
  75.7 4.7 collective-permute-start.10
  91.1 6.7 %collective-permute-start.24 = (f32[2]{0:T(128)S(1)}, f32[2]{0:T(128)S(1)}, u32[]{:S(2)}, u32[]{:S(2)}) collective-permute-start(f32[2]{0:T(128)S(1)} %get-tuple-element.322), channel_id=1, source_target_pairs={{0,8},{8,0},{16,24},{24,16},{32,40},{40,32},{48,56},{56,48},{1,9},... | collective-permute-start | bytes 32 | tf_op jit(solution)/shard_map/ppermute | solution.py:41
  113.0 7.2 %collective-permute-start.31 = (f32[1,2,1,256]{3,2,1,0:T(1,128)S(1)}, f32[1,2,1,256]{3,2,1,0:T(1,128)S(1)}, u32[]{:S(2)}, u32[]{:S(2)}) collective-permute-start(f32[1,2,1,256]{3,2,1,0:T(1,128)S(1)} %get-tuple-element.409), channel_id=1, source_target_pairs={{8,0},{16,8},{24,16},{32,24},{40,32},{48,40},{56,48},{0,56},{9,1},... | collective-permute-start | bytes 6152 | tf_op jit(solution)/shard_map/ppermute | solution.py:30
  120.3 5.4 collective-permute-start.33
  125.9 5.0 collective-permute-start.34
  146.1 6.9 %collective-permute-start.40 = (f32[2]{0:T(128)S(1)}, f32[2]{0:T(128)S(1)}, u32[]{:S(2)}, u32[]{:S(2)}) collective-permute-start(f32[2]{0:T(128)S(1)} %multiply_reduce_fusion.5), channel_id=1, source_target_pairs={{0,8},{8,0},{16,24},{24,16},{32,40},{40,32},{48,56},{56,48},{1,9},... | collective-permute-start | bytes 32 | tf_op jit(solution)/shard_map/ppermute | solution.py:41
  168.6 9.7 %collective-permute-start.47 = (f32[1,2,1,256]{3,2,1,0:T(1,128)S(1)}, f32[1,2,1,256]{3,2,1,0:T(1,128)S(1)}, u32[]{:S(2)}, u32[]{:S(2)}) collective-permute-start(f32[1,2,1,256]{3,2,1,0:T(1,128)S(1)} %get-tuple-element.405), channel_id=1, source_target_pairs={{8,0},{16,8},{24,16},{32,24},{40,32},{48,40},{56,48},{0,56},{9,1},... | collective-permute-start | bytes 6152 | tf_op jit(solution)/shard_map/ppermute | solution.py:30
  179.1 8.4 %collective-permute-start.49 = (f32[1,2,66,1]{3,2,1,0:T(8,128)}, f32[1,2,66,1]{3,2,1,0:T(8,128)}, u32[]{:S(2)}, u32[]{:S(2)}) collective-permute-start(f32[1,2,66,1]{3,2,1,0:T(8,128)} %get-tuple-element.376), channel_id=1, source_target_pairs={{0,1},{1,2},{2,3},{3,4},{4,5},{5,6},{6,7},{7,0},{8,9},{9,10},{10,1... | collective-permute-start | bytes 1592 | tf_op jit(solution)/shard_map/ppermute | solution.py:27
  180.0 7.6 %collective-permute-start.48 = (f32[1,2,66,1]{3,2,1,0:T(8,128)}, f32[1,2,66,1]{3,2,1,0:T(8,128)}, u32[]{:S(2)}, u32[]{:S(2)}) collective-permute-start(f32[1,2,66,1]{3,2,1,0:T(8,128)} %get-tuple-element.375), channel_id=1, source_target_pairs={{1,0},{2,1},{3,2},{4,3},{5,4},{6,5},{7,6},{0,7},{9,8},{10,9},{11,1... | collective-permute-start | bytes 1592 | tf_op jit(solution)/shard_map/ppermute | solution.py:30
  207.4 9.6 %collective-permute-start.56 = (f32[1,2,1,256]{3,2,1,0:T(1,128)S(1)}, f32[1,2,1,256]{3,2,1,0:T(1,128)S(1)}, u32[]{:S(2)}, u32[]{:S(2)}) collective-permute-start(f32[1,2,1,256]{3,2,1,0:T(1,128)S(1)} %get-tuple-element.401), channel_id=1, source_target_pairs={{0,8},{8,16},{16,24},{24,32},{32,40},{40,48},{48,56},{56,0},{1,9},... | collective-permute-start | bytes 6152 | tf_op jit(solution)/shard_map/ppermute | solution.py:27
  217.1 5.4 collective-permute-start.59
  217.2 5.3 collective-permute-start.58
  228.0 5.0 collective-permute-start.61
  238.4 15.0 %collective-permute-start.63 = (f32[5,2,4,66,1]{3,2,4,1,0:T(4,128)}, f32[5,2,4,66,1]{3,2,4,1,0:T(4,128)}, u32[]{:S(2)}, u32[]{:S(2)}) collective-permute-start(f32[5,2,4,66,1]{3,2,4,1,0:T(4,128)} %copy.20), channel_id=1, source_target_pairs={{0,1},{1,2},{2,3},{3,4},{4,5},{5,6},{6,7},{7,0},{8,9},{9,10},{10,1... | collective-permute-start | bytes 31688 | tf_op jit(solution)/shard_map/ppermute | solution.py:27
  240.9 15.0 %collective-permute-start.62 = (f32[5,2,4,66,1]{3,2,4,1,0:T(4,128)}, f32[5,2,4,66,1]{3,2,4,1,0:T(4,128)}, u32[]{:S(2)}, u32[]{:S(2)}) collective-permute-start(f32[5,2,4,66,1]{3,2,4,1,0:T(4,128)} %copy.18), channel_id=1, source_target_pairs={{1,0},{2,1},{3,2},{4,3},{5,4},{6,5},{7,6},{0,7},{9,8},{10,9},{11,1... | collective-permute-start | bytes 31688 | tf_op jit(solution)/shard_map/ppermute | solution.py:30
  264.9 4.6 collective-permute-start.65
  270.6 7.3 %collective-permute-start.67 = (f32[2,2,66,1]{3,2,1,0:T(8,128)}, f32[2,2,66,1]{3,2,1,0:T(8,128)}, u32[]{:S(2)}, u32[]{:S(2)}) collective-permute-start(f32[2,2,66,1]{3,2,1,0:T(8,128)} %get-tuple-element.354), channel_id=1, source_target_pairs={{0,1},{1,2},{2,3},{3,4},{4,5},{5,6},{6,7},{7,0},{8,9},{9,10},{10,1... | collective-permute-start | bytes 3176 | tf_op jit(solution)/shard_map/ppermute | solution.py:27
  270.6 7.3 %collective-permute-start.66 = (f32[2,2,66,1]{3,2,1,0:T(8,128)}, f32[2,2,66,1]{3,2,1,0:T(8,128)}, u32[]{:S(2)}, u32[]{:S(2)}) collective-permute-start(f32[2,2,66,1]{3,2,1,0:T(8,128)} %get-tuple-element.353), channel_id=1, source_target_pairs={{1,0},{2,1},{3,2},{4,3},{5,4},{6,5},{7,6},{0,7},{9,8},{10,9},{11,1... | collective-permute-start | bytes 3176 | tf_op jit(solution)/shard_map/ppermute | solution.py:30
  279.2 4.5 collective-permute-start.75
  284.8 7.5 %collective-permute-start.77 = (f32[1,2,66,1]{3,2,1,0:T(8,128)}, f32[1,2,66,1]{3,2,1,0:T(8,128)}, u32[]{:S(2)}, u32[]{:S(2)}) collective-permute-start(f32[1,2,66,1]{3,2,1,0:T(8,128)} %get-tuple-element.372), channel_id=1, source_target_pairs={{0,1},{1,2},{2,3},{3,4},{4,5},{5,6},{6,7},{7,0},{8,9},{9,10},{10,1... | collective-permute-start | bytes 1592 | tf_op jit(solution)/shard_map/ppermute | solution.py:27
  284.8 8.1 %collective-permute-start.76 = (f32[1,2,66,1]{3,2,1,0:T(8,128)}, f32[1,2,66,1]{3,2,1,0:T(8,128)}, u32[]{:S(2)}, u32[]{:S(2)}) collective-permute-start(f32[1,2,66,1]{3,2,1,0:T(8,128)} %get-tuple-element.371), channel_id=1, source_target_pairs={{1,0},{2,1},{3,2},{4,3},{5,4},{6,5},{7,6},{0,7},{9,8},{10,9},{11,1... | collective-permute-start | bytes 1592 | tf_op jit(solution)/shard_map/ppermute | solution.py:30
  294.3 4.7 collective-permute-start.78
  316.1 7.3 %collective-permute-start.84 = (f32[2]{0:T(128)S(1)}, f32[2]{0:T(128)S(1)}, u32[]{:S(2)}, u32[]{:S(2)}) collective-permute-start(f32[2]{0:T(128)S(1)} %get-tuple-element.307), channel_id=1, source_target_pairs={{0,8},{8,0},{16,24},{24,16},{32,40},{40,32},{48,56},{56,48},{1,9},... | collective-permute-start | bytes 32 | tf_op jit(solution)/shard_map/ppermute | solution.py:41
  339.0 7.5 %collective-permute-start.91 = (f32[1,2,1,256]{3,2,1,0:T(1,128)S(1)}, f32[1,2,1,256]{3,2,1,0:T(1,128)S(1)}, u32[]{:S(2)}, u32[]{:S(2)}) collective-permute-start(f32[1,2,1,256]{3,2,1,0:T(1,128)S(1)} %get-tuple-element.395), channel_id=1, source_target_pairs={{8,0},{16,8},{24,16},{32,24},{40,32},{48,40},{56,48},{0,56},{9,1},... | collective-permute-start | bytes 6152 | tf_op jit(solution)/shard_map/ppermute | solution.py:30
  347.2 8.1 %collective-permute-start.93 = (f32[1,2,66,1]{3,2,1,0:T(8,128)}, f32[1,2,66,1]{3,2,1,0:T(8,128)}, u32[]{:S(2)}, u32[]{:S(2)}) collective-permute-start(f32[1,2,66,1]{3,2,1,0:T(8,128)} %get-tuple-element.370), channel_id=1, source_target_pairs={{0,1},{1,2},{2,3},{3,4},{4,5},{5,6},{6,7},{7,0},{8,9},{9,10},{10,1... | collective-permute-start | bytes 1592 | tf_op jit(solution)/shard_map/ppermute | solution.py:27
  348.2 7.1 %collective-permute-start.92 = (f32[1,2,66,1]{3,2,1,0:T(8,128)}, f32[1,2,66,1]{3,2,1,0:T(8,128)}, u32[]{:S(2)}, u32[]{:S(2)}) collective-permute-start(f32[1,2,66,1]{3,2,1,0:T(8,128)} %get-tuple-element.369), channel_id=1, source_target_pairs={{1,0},{2,1},{3,2},{4,3},{5,4},{6,5},{7,6},{0,7},{9,8},{10,9},{11,1... | collective-permute-start | bytes 1592 | tf_op jit(solution)/shard_map/ppermute | solution.py:30
  356.6 4.2 collective-permute-start.94
  377.6 6.9 %collective-permute-start.100 = (f32[2]{0:T(128)S(1)}, f32[2]{0:T(128)S(1)}, u32[]{:S(2)}, u32[]{:S(2)}) collective-permute-start(f32[2]{0:T(128)S(1)} %multiply_reduce_fusion), channel_id=1, source_target_pairs={{0,8},{8,0},{16,24},{24,16},{32,40},{40,32},{48,56},{56,48},{1,9},... | collective-permute-start | bytes 32 | tf_op jit(solution)/shard_map/ppermute | solution.py:41
  401.6 6.9 %collective-permute-start.107 = (f32[1,2,1,256]{3,2,1,0:T(1,128)S(1)}, f32[1,2,1,256]{3,2,1,0:T(1,128)S(1)}, u32[]{:S(2)}, u32[]{:S(2)}) collective-permute-start(f32[1,2,1,256]{3,2,1,0:T(1,128)S(1)} %get-tuple-element.391), channel_id=1, source_target_pairs={{8,0},{16,8},{24,16},{32,24},{40,32},{48,40},{56,48},{0,56},{9,1},... | collective-permute-start | bytes 6152 | tf_op jit(solution)/shard_map/ppermute | solution.py:30
  409.6 8.1 %collective-permute-start.109 = (f32[1,2,66,1]{3,2,1,0:T(8,128)}, f32[1,2,66,1]{3,2,1,0:T(8,128)}, u32[]{:S(2)}, u32[]{:S(2)}) collective-permute-start(f32[1,2,66,1]{3,2,1,0:T(8,128)} %get-tuple-element.368), channel_id=1, source_target_pairs={{0,1},{1,2},{2,3},{3,4},{4,5},{5,6},{6,7},{7,0},{8,9},{9,10},{10,1... | collective-permute-start | bytes 1592 | tf_op jit(solution)/shard_map/ppermute | solution.py:27
  409.6 8.1 %collective-permute-start.108 = (f32[1,2,66,1]{3,2,1,0:T(8,128)}, f32[1,2,66,1]{3,2,1,0:T(8,128)}, u32[]{:S(2)}, u32[]{:S(2)}) collective-permute-start(f32[1,2,66,1]{3,2,1,0:T(8,128)} %get-tuple-element.367), channel_id=1, source_target_pairs={{1,0},{2,1},{3,2},{4,3},{5,4},{6,5},{7,6},{0,7},{9,8},{10,9},{11,1... | collective-permute-start | bytes 1592 | tf_op jit(solution)/shard_map/ppermute | solution.py:30
  419.2 4.5 collective-permute-start.110
  440.4 6.9 %collective-permute-start.117 = (f32[1,2,1,256]{3,2,1,0:T(1,128)S(1)}, f32[1,2,1,256]{3,2,1,0:T(1,128)S(1)}, u32[]{:S(2)}, u32[]{:S(2)}) collective-permute-start(f32[1,2,1,256]{3,2,1,0:T(1,128)S(1)} %get-tuple-element.388), channel_id=1, source_target_pairs={{8,0},{16,8},{24,16},{32,24},{40,32},{48,40},{56,48},{0,56},{9,1},... | collective-permute-start | bytes 6152 | tf_op jit(solution)/shard_map/ppermute | solution.py:30
  447.7 5.4 collective-permute-start.119
  447.8 5.3 collective-permute-start.118
  469.1 8.9 %collective-permute-start.122 = (f32[2,4,64]{2,1,0:T(4,128)S(1)}, f32[2,4,64]{2,1,0:T(4,128)S(1)}, u32[]{:S(2)}, u32[]{:S(2)}) collective-permute-start(f32[2,4,64]{2,1,0:T(4,128)S(1)} %add.751), channel_id=1, source_target_pairs={{0,4},{1,5},{2,6},{3,7},{4,0},{5,1},{6,2},{7,3},{8,12},{9,13},{10,... | collective-permute-start | bytes 6152 | tf_op jit(solution)/shard_map/ppermute | solution.py:41
  478.6 10.1 %collective-permute-start.123 = (f32[2]{0:T(128)S(1)}, f32[2]{0:T(128)S(1)}, u32[]{:S(2)}, u32[]{:S(2)}) collective-permute-start(f32[2]{0:T(128)S(1)} %broadcast_multiply_fusion.9), channel_id=1, source_target_pairs={{0,8},{8,0},{16,24},{24,16},{32,40},{40,32},{48,56},{56,48},{1,9},... | collective-permute-start | bytes 32 | tf_op jit(solution)/shard_map/ppermute | solution.py:41
  491.5 4.3 collective-permute-start.125
  (133 other events, 726.2 us)
Sparse Core Ops, SparseCore 0:
  464.0 64.6 all-gather.1
where the time goes:
time: 553 us; the launch traced here: 543 us
  starting transfers between devices  207 us (37%)
  waiting for transfers between devices  172 us (31%)
  other arithmetic  72 us (13%)
  local copies, waits for them, and re-layouts  63.5 us (11%)
  between operations  16.6 us (3%)
  blocking collectives  11.7 us (2%)
    ppermute x78, waiting for transfers between devices, tree_sum(): values = values + lax.ppermute(values, axis, pairs)  128 us
    ppermute x78, starting transfers between devices, tree_sum(): values = values + lax.ppermute(values, axis, pairs)  104 us
    ppermute x24, starting transfers between devices, padded_2(): lax.ppermute(lax.slice_in_dim(block, 0, width, axis=dim), axis, backward)  91.6 us
    all_gather x1, waiting for transfers between devices, shards(): lax.all_gather(state_stack, 'member', axis=1, tiled=True)  23.3 us
    another operation x12, local copies, waits for them, and re-layouts, split_rims(): south_side = south_side.at[..., 0, :].multiply(south_keep)  13.3 us
    slice x22, local copies, waits for them, and re-layouts, padded_2(): lax.slice_in_dim(block, 0, width, axis=dim)  12.8 us
    ppermute x24, starting transfers between devices, padded_2(): lax.ppermute(lax.slice_in_dim(block, block.shape[dim] - width, None, axis...  12.2 us
    another operation x12, local copies, waits for them, and re-layouts, split_rims(): north_side = north_side.at[..., -1, :].multiply(north_keep)  11.5 us
  transfers between devices with their start and end apart: 127, of which 99 were waited for; matrix products, arithmetic and copies ran while one was open for 11% of the time, Pallas kernels for 0%

commit v1 on v0

--- a/solution.py
+++ b/solution.py
@@ -167,7 +167,10 @@
     score = tree_sum(jnp.sum(overturn * lat_weight, axis=(1, 2)) * score_scale, ("gridy",))
     state_stack = jnp.stack((temp, salt, uvel, vvel))
     every_state, every_eta, every_score = (
-        lax.all_gather(state_stack, "member", axis=1, tiled=True),
+        jnp.concatenate(
+            lax.all_to_all(jnp.stack([state_stack] * lax.axis_size("member")), "member", 0, 0),
+            axis=1,
+        ),
         lax.all_gather(eta, "member", axis=0, tiled=True),
         lax.all_gather(score, "member", axis=0, tiled=True),
     )

time: 553 us -> 722 us (1.31)
  other arithmetic: 72 us -> 190 us
  local copies, waits for them, and re-layouts: 63.5 us -> 92.9 us
  starting transfers between devices: 207 us -> 233 us
  between operations: 16.6 us -> 3.15 us
    another operation x2 -> x4, other arithmetic: 0.39 us -> 79.9 us  [pressure(): return PRESS_K * jnp.cumsum(BETA_S * salt - ALPHA_T * temp, axis=-3)]
    all_gather x1 -> x0, waiting for transfers between devices: 23.3 us -> none  [shards(): lax.all_gather(state_stack, 'member', axis=1, tiled=True)]
    ppermute x24, waiting for transfers between devices: 10.5 us -> 32.9 us  [padded_2(): lax.ppermute(lax.slice_in_dim(block, 0, width, axis=dim), axis, backward)]
    ppermute x78, starting transfers between devices: 104 us -> 119 us  [tree_sum(): values = values + lax.ppermute(values, axis, pairs)]
    ppermute x78, waiting for transfers between devices: 128 us -> 142 us  [tree_sum(): values = values + lax.ppermute(values, axis, pairs)]
    another operation x12 -> x10, local copies, waits for them, and re-layouts: 11.5 us -> 19.7 us  [split_rims(): north_side = north_side.at[..., -1, :].multiply(north_keep)]
    ppermute x24, waiting for transfers between devices: 10.2 us -> 2.95 us  [padded_2(): lax.ppermute(lax.slice_in_dim(block, block.shape[dim] - width, None, axis...]
    another operation x12 -> x10, local copies, waits for them, and re-layouts: 13.3 us -> 17.3 us  [split_rims(): south_side = south_side.at[..., 0, :].multiply(south_keep)]
  transfers between devices with their start and end apart: 127 -> 127, of which waited for: 99 -> 93; matrix products, arithmetic and copies ran while one was open for 11% -> 17% of each run, Pallas kernels for 0% -> 0%
where the time goes in v1:
time: 722 us; the launch traced here: 709 us
  starting transfers between devices  233 us (32%)
  other arithmetic  190 us (26%)
  waiting for transfers between devices  178 us (25%)
  local copies, waits for them, and re-layouts  92.9 us (13%)
  blocking collectives  11.7 us (2%)
    ppermute x78, waiting for transfers between devices, tree_sum(): values = values + lax.ppermute(values, axis, pairs)  142 us
    ppermute x78, starting transfers between devices, tree_sum(): values = values + lax.ppermute(values, axis, pairs)  119 us
    ppermute x24, starting transfers between devices, padded_2(): lax.ppermute(lax.slice_in_dim(block, 0, width, axis=dim), axis, backward)  95.2 us
    another operation x4, other arithmetic, pressure(): return PRESS_K * jnp.cumsum(BETA_S * salt - ALPHA_T * temp, axis=-3)  79.9 us
    ppermute x24, waiting for transfers between devices, padded_2(): lax.ppermute(lax.slice_in_dim(block, 0, width, axis=dim), axis, backward)  32.9 us
    another operation x10, local copies, waits for them, and re-layouts, split_rims(): north_side = north_side.at[..., -1, :].multiply(north_keep)  19.7 us
    another operation x10, local copies, waits for them, and re-layouts, split_rims(): south_side = south_side.at[..., 0, :].multiply(south_keep)  17.3 us
  transfers between devices with their start and end apart: 127, of which 93 were waited for; matrix products, arithmetic and copies ran while one was open for 17% of the time, Pallas kernels for 0%

profile of v1, /device:TPU:1, one launch (start us, length us, event | category | flops | bytes accessed | tf_op | source)
XLA Modules:
  0.0 709.2 jit_solution(9211693679718649728)
XLA Ops:
  6.1 35.3 %reduce_window_sum.33 = f32[1,2,4,64,256]{4,2,3,1,0:T(4,128)} reduce-window(f32[1,2,4,64,256]{4,2,3,1,0:T(4,128)} %subtract_bitcast_fusion.1, f32[]{:T(128)} %constant.599.clone.1), window={size=1x1x4x1x1 pad=0_0x0_0x3_0x0_0x0_0}, to_apply=%region_0.0 | reduce-window | flops 393216 | bytes 1048580 | tf_op jit(solution)/shard_map/jit(cumsum)/reduce_window_sum | solution.py:47
  55.2 3.7 collective-permute-start.2
  66.1 5.4 fusion.172
  72.5 6.3 fusion.170
  81.8 4.2 collective-permute-start.5
  93.9 3.6 collective-permute-start.6
  108.9 4.3 collective-permute-start.15
  117.1 3.6 collective-permute-start.16
  128.6 4.3 collective-permute-start.18
  149.3 6.1 collective-permute-start.24
  172.1 5.9 collective-permute-start.31
  179.3 6.5 subtract_bitcast_fusion
  186.0 3.5 collective-permute-start.32
  209.0 6.0 collective-permute-start.40
  231.0 6.1 collective-permute-start.47
  242.6 4.0 collective-permute-start.48
  269.1 3.6 collective-permute-done.55
  273.7 5.9 collective-permute-start.56
  279.9 35.4 %reduce_window_sum.35 = f32[1,2,4,64,256]{4,2,3,1,0:T(4,128)} reduce-window(f32[1,2,4,64,256]{4,2,3,1,0:T(4,128)} %get-tuple-element.323, f32[]{:T(128)} %constant.599.clone.1), window={size=1x1x4x1x1 pad=0_0x0_0x3_0x0_0x0_0}, to_apply=%region_9.10 | reduce-window | flops 393216 | bytes 1048580 | tf_op jit(solution)/shard_map/jit(cumsum)/reduce_window_sum | solution.py:47
  316.2 3.6 collective-permute-start.58
  335.9 3.6 collective-permute-start.61
  348.7 3.8 collective-permute-start.62
  361.8 4.8 fusion.162
  368.3 5.8 fusion.160
  376.6 3.7 collective-permute-start.65
  380.3 5.9 collective-permute-done.65
  388.0 3.6 collective-permute-start.66
  401.2 4.3 collective-permute-start.75
  409.5 3.6 collective-permute-start.76
  421.2 4.3 collective-permute-start.78
  441.9 6.0 collective-permute-start.84
  464.5 6.0 collective-permute-start.91
  471.9 4.3 collective-permute-done.91
  476.9 3.6 collective-permute-start.92
  508.0 6.1 collective-permute-start.100
  532.2 6.1 collective-permute-start.107
  538.5 4.3 collective-permute-done.107
  543.7 3.6 collective-permute-start.108
  575.9 6.1 collective-permute-start.117
  581.9 4.0 collective-permute-done.117
  586.0 3.5 collective-permute-start.118
  601.6 4.2 fusion.79
  613.2 5.7 all-to-all-start
  619.1 43.0 %collective-permute-done.120 = f32[2,4,64]{1,2,0:T(8,128)S(1)} collective-permute-done((f32[2,4,64]{1,2,0:T(8,128)S(1)}, f32[2,4,64]{1,2,0:T(8,128)S(1)}, u32[]{:S(2)}, u32[]{:S(2)}) %collective-permute-start.120) | collective-permute-done | bytes 2080 | tf_op jit(solution)/shard_map/ppermute | solution.py:41
  668.6 6.1 all_gather.6
  675.8 7.4 %collective-permute-start.123 = (f32[2]{0:T(128)S(1)}, f32[2]{0:T(128)S(1)}, u32[]{:S(2)}, u32[]{:S(2)}) collective-permute-start(f32[2]{0:T(128)S(1)} %broadcast_multiply_fusion.5), channel_id=1, source_target_pairs={{0,8},{8,0},{16,24},{24,16},{32,40},{40,32},{48,56},{56,48},{1,9},... | collective-permute-start | bytes 32 | tf_op jit(solution)/shard_map/ppermute | solution.py:41
  691.1 5.6 all-reduce
  699.8 4.8 copy.544
  (548 shorter events, 375.4 us)
Async XLA Ops:
  52.0 10.7 %collective-permute-start.3 = (f32[5,2,4,66,1]{3,2,4,1,0:T(4,128)S(1)}, f32[5,2,4,66,1]{3,2,4,1,0:T(4,128)S(1)}, u32[]{:S(2)}, u32[]{:S(2)}) collective-permute-start(f32[5,2,4,66,1]{3,2,4,1,0:T(4,128)S(1)} %copy.454), channel_id=1, source_target_pairs={{0,1},{1,2},{2,3},{3,4},{4,5},{5,6},{6,7},{7,0},{8,9},{9,10},{10,1... | collective-permute-start | bytes 31688 | tf_op jit(solution)/shard_map/ppermute | solution.py:27
  55.2 9.2 %collective-permute-start.2 = (f32[5,2,4,66,1]{3,2,4,1,0:T(4,128)S(1)}, f32[5,2,4,66,1]{3,2,4,1,0:T(4,128)S(1)}, u32[]{:S(2)}, u32[]{:S(2)}) collective-permute-start(f32[5,2,4,66,1]{3,2,4,1,0:T(4,128)S(1)} %copy.452), channel_id=1, source_target_pairs={{1,0},{2,1},{3,2},{4,3},{5,4},{6,5},{7,6},{0,7},{9,8},{10,9},{11,1... | collective-permute-start | bytes 31688 | tf_op jit(solution)/shard_map/ppermute | solution.py:30
  81.8 9.4 %collective-permute-start.5 = (f32[2,2,1,256]{2,3,1,0:T(8,128)}, f32[2,2,1,256]{2,3,1,0:T(8,128)S(1)}, u32[]{:S(2)}, u32[]{:S(2)}) collective-permute-start(f32[2,2,1,256]{2,3,1,0:T(8,128)} %get-tuple-element.391), channel_id=1, source_target_pairs={{8,0},{16,8},{24,16},{32,24},{40,32},{48,40},{56,48},{0,56},{9,1},... | collective-permute-start | bytes 12296 | tf_op jit(solution)/shard_map/ppermute | solution.py:30
  86.0 6.4 collective-permute-start.4
  93.9 13.1 %collective-permute-start.7 = (f32[2,2,66,1]{2,3,1,0:T(1,128)}, f32[2,2,66,1]{2,3,1,0:T(1,128)}, u32[]{:S(2)}, u32[]{:S(2)}) collective-permute-start(f32[2,2,66,1]{2,3,1,0:T(1,128)} %get-tuple-element.360), channel_id=1, source_target_pairs={{0,1},{1,2},{2,3},{3,4},{4,5},{5,6},{6,7},{7,0},{8,9},{9,10},{10,1... | collective-permute-start | bytes 3176 | tf_op jit(solution)/shard_map/ppermute | solution.py:27
  93.9 13.1 %collective-permute-start.6 = (f32[2,2,66,1]{2,3,1,0:T(1,128)}, f32[2,2,66,1]{2,3,1,0:T(1,128)}, u32[]{:S(2)}, u32[]{:S(2)}) collective-permute-start(f32[2,2,66,1]{2,3,1,0:T(1,128)} %get-tuple-element.359), channel_id=1, source_target_pairs={{1,0},{2,1},{3,2},{4,3},{5,4},{6,5},{7,6},{0,7},{9,8},{10,9},{11,1... | collective-permute-start | bytes 3176 | tf_op jit(solution)/shard_map/ppermute | solution.py:30
  108.9 7.1 %collective-permute-start.15 = (f32[1,2,1,256]{2,3,1,0:T(8,128)S(1)}, f32[1,2,1,256]{2,3,1,0:T(8,128)S(1)}, u32[]{:S(2)}, u32[]{:S(2)}) collective-permute-start(f32[1,2,1,256]{2,3,1,0:T(8,128)S(1)} %get-tuple-element.419), channel_id=1, source_target_pairs={{8,0},{16,8},{24,16},{32,24},{40,32},{48,40},{56,48},{0,56},{9,1},... | collective-permute-start | bytes 6152 | tf_op jit(solution)/shard_map/ppermute | solution.py:30
  117.1 9.9 %collective-permute-start.17 = (f32[1,2,66,1]{2,3,1,0:T(1,128)}, f32[1,2,66,1]{2,3,1,0:T(1,128)}, u32[]{:S(2)}, u32[]{:S(2)}) collective-permute-start(f32[1,2,66,1]{2,3,1,0:T(1,128)} %get-tuple-element.376), channel_id=1, source_target_pairs={{0,1},{1,2},{2,3},{3,4},{4,5},{5,6},{6,7},{7,0},{8,9},{9,10},{10,1... | collective-permute-start | bytes 1592 | tf_op jit(solution)/shard_map/ppermute | solution.py:27
  117.1 9.9 %collective-permute-start.16 = (f32[1,2,66,1]{2,3,1,0:T(1,128)}, f32[1,2,66,1]{2,3,1,0:T(1,128)}, u32[]{:S(2)}, u32[]{:S(2)}) collective-permute-start(f32[1,2,66,1]{2,3,1,0:T(1,128)} %get-tuple-element.375), channel_id=1, source_target_pairs={{1,0},{2,1},{3,2},{4,3},{5,4},{6,5},{7,6},{0,7},{9,8},{10,9},{11,1... | collective-permute-start | bytes 1592 | tf_op jit(solution)/shard_map/ppermute | solution.py:30
  128.6 5.1 collective-permute-start.18
  149.3 6.9 collective-permute-start.24
  172.1 13.7 %collective-permute-start.31 = (f32[1,2,1,256]{2,3,1,0:T(8,128)S(1)}, f32[1,2,1,256]{2,3,1,0:T(8,128)S(1)}, u32[]{:S(2)}, u32[]{:S(2)}) collective-permute-start(f32[1,2,1,256]{2,3,1,0:T(8,128)S(1)} %get-tuple-element.415), channel_id=1, source_target_pairs={{8,0},{16,8},{24,16},{32,24},{40,32},{48,40},{56,48},{0,56},{9,1},... | collective-permute-start | bytes 6152 | tf_op jit(solution)/shard_map/ppermute | solution.py:30
  178.0 7.8 %collective-permute-start.30 = (f32[1,2,1,256]{2,3,1,0:T(8,128)S(1)}, f32[1,2,1,256]{2,3,1,0:T(8,128)S(1)}, u32[]{:S(2)}, u32[]{:S(2)}) collective-permute-start(f32[1,2,1,256]{2,3,1,0:T(8,128)S(1)} %get-tuple-element.416), channel_id=1, source_target_pairs={{0,8},{8,16},{16,24},{24,32},{32,40},{40,48},{48,56},{56,0},{1,9},... | collective-permute-start | bytes 6152 | tf_op jit(solution)/shard_map/ppermute | solution.py:27
  185.9 5.2 collective-permute-start.33
  186.0 5.1 collective-permute-start.32
  209.0 6.8 collective-permute-start.40
  231.0 11.5 %collective-permute-start.47 = (f32[1,2,1,256]{2,3,1,0:T(8,128)S(1)}, f32[1,2,1,256]{2,3,1,0:T(8,128)S(1)}, u32[]{:S(2)}, u32[]{:S(2)}) collective-permute-start(f32[1,2,1,256]{2,3,1,0:T(8,128)S(1)} %get-tuple-element.411), channel_id=1, source_target_pairs={{8,0},{16,8},{24,16},{32,24},{40,32},{48,40},{56,48},{0,56},{9,1},... | collective-permute-start | bytes 6152 | tf_op jit(solution)/shard_map/ppermute | solution.py:30
  237.1 5.4 collective-permute-start.46
  242.6 10.4 %collective-permute-start.49 = (f32[1,2,66,1]{2,3,1,0:T(1,128)S(1)}, f32[1,2,66,1]{2,3,1,0:T(1,128)S(1)}, u32[]{:S(2)}, u32[]{:S(2)}) collective-permute-start(f32[1,2,66,1]{2,3,1,0:T(1,128)S(1)} %get-tuple-element.372), channel_id=1, source_target_pairs={{0,1},{1,2},{2,3},{3,4},{4,5},{5,6},{6,7},{7,0},{8,9},{9,10},{10,1... | collective-permute-start | bytes 1592 | tf_op jit(solution)/shard_map/ppermute | solution.py:27
  242.6 10.3 %collective-permute-start.48 = (f32[1,2,66,1]{2,3,1,0:T(1,128)S(1)}, f32[1,2,66,1]{2,3,1,0:T(1,128)S(1)}, u32[]{:S(2)}, u32[]{:S(2)}) collective-permute-start(f32[1,2,66,1]{2,3,1,0:T(1,128)S(1)} %get-tuple-element.371), channel_id=1, source_target_pairs={{1,0},{2,1},{3,2},{4,3},{5,4},{6,5},{7,6},{0,7},{9,8},{10,9},{11,1... | collective-permute-start | bytes 1592 | tf_op jit(solution)/shard_map/ppermute | solution.py:30
  273.7 41.5 %collective-permute-start.56 = (f32[1,2,1,256]{2,3,1,0:T(8,128)}, f32[1,2,1,256]{2,3,1,0:T(8,128)S(1)}, u32[]{:S(2)}, u32[]{:S(2)}) collective-permute-start(f32[1,2,1,256]{2,3,1,0:T(8,128)} %get-tuple-element.407), channel_id=1, source_target_pairs={{0,8},{8,16},{16,24},{24,32},{32,40},{40,48},{48,56},{56,0},{1,9},... | collective-permute-start | bytes 6152 | tf_op jit(solution)/shard_map/ppermute | solution.py:27
  279.6 35.6 %collective-permute-start.57 = (f32[1,2,1,256]{2,3,1,0:T(8,128)}, f32[1,2,1,256]{2,3,1,0:T(8,128)S(1)}, u32[]{:S(2)}, u32[]{:S(2)}) collective-permute-start(f32[1,2,1,256]{2,3,1,0:T(8,128)} %get-tuple-element.408), channel_id=1, source_target_pairs={{8,0},{16,8},{24,16},{32,24},{40,32},{48,40},{56,48},{0,56},{9,1},... | collective-permute-start | bytes 6152 | tf_op jit(solution)/shard_map/ppermute | solution.py:30
  316.2 5.0 collective-permute-start.59
  346.3 10.7 %collective-permute-start.63 = (f32[5,2,4,66,1]{3,2,4,1,0:T(4,128)}, f32[5,2,4,66,1]{3,2,4,1,0:T(4,128)}, u32[]{:S(2)}, u32[]{:S(2)}) collective-permute-start(f32[5,2,4,66,1]{3,2,4,1,0:T(4,128)} %copy.511), channel_id=1, source_target_pairs={{0,1},{1,2},{2,3},{3,4},{4,5},{5,6},{6,7},{7,0},{8,9},{9,10},{10,1... | collective-permute-start | bytes 31688 | tf_op jit(solution)/shard_map/ppermute | solution.py:27
  348.7 10.7 %collective-permute-start.62 = (f32[5,2,4,66,1]{3,2,4,1,0:T(4,128)}, f32[5,2,4,66,1]{3,2,4,1,0:T(4,128)}, u32[]{:S(2)}, u32[]{:S(2)}) collective-permute-start(f32[5,2,4,66,1]{3,2,4,1,0:T(4,128)} %copy.509), channel_id=1, source_target_pairs={{1,0},{2,1},{3,2},{4,3},{5,4},{6,5},{7,6},{0,7},{9,8},{10,9},{11,1... | collective-permute-start | bytes 31688 | tf_op jit(solution)/shard_map/ppermute | solution.py:30
  376.6 9.7 %collective-permute-start.65 = (f32[2,2,1,256]{2,3,1,0:T(8,128)S(1)}, f32[2,2,1,256]{2,3,1,0:T(8,128)S(1)}, u32[]{:S(2)}, u32[]{:S(2)}) collective-permute-start(f32[2,2,1,256]{2,3,1,0:T(8,128)S(1)} %get-tuple-element.384), channel_id=1, source_target_pairs={{8,0},{16,8},{24,16},{32,24},{40,32},{48,40},{56,48},{0,56},{9,1},... | collective-permute-start | bytes 12296 | tf_op jit(solution)/shard_map/ppermute | solution.py:30
  380.3 6.1 collective-permute-start.64
  388.0 11.1 %collective-permute-start.67 = (f32[2,2,66,1]{2,3,1,0:T(1,128)}, f32[2,2,66,1]{2,3,1,0:T(1,128)}, u32[]{:S(2)}, u32[]{:S(2)}) collective-permute-start(f32[2,2,66,1]{2,3,1,0:T(1,128)} %get-tuple-element.358), channel_id=1, source_target_pairs={{0,1},{1,2},{2,3},{3,4},{4,5},{5,6},{6,7},{7,0},{8,9},{9,10},{10,1... | collective-permute-start | bytes 3176 | tf_op jit(solution)/shard_map/ppermute | solution.py:27
  388.0 11.1 %collective-permute-start.66 = (f32[2,2,66,1]{2,3,1,0:T(1,128)}, f32[2,2,66,1]{2,3,1,0:T(1,128)}, u32[]{:S(2)}, u32[]{:S(2)}) collective-permute-start(f32[2,2,66,1]{2,3,1,0:T(1,128)} %get-tuple-element.357), channel_id=1, source_target_pairs={{1,0},{2,1},{3,2},{4,3},{5,4},{6,5},{7,6},{0,7},{9,8},{10,9},{11,1... | collective-permute-start | bytes 3176 | tf_op jit(solution)/shard_map/ppermute | solution.py:30
  401.2 7.1 %collective-permute-start.75 = (f32[1,2,1,256]{2,3,1,0:T(8,128)S(1)}, f32[1,2,1,256]{2,3,1,0:T(8,128)S(1)}, u32[]{:S(2)}, u32[]{:S(2)}) collective-permute-start(f32[1,2,1,256]{2,3,1,0:T(8,128)S(1)} %get-tuple-element.405), channel_id=1, source_target_pairs={{8,0},{16,8},{24,16},{32,24},{40,32},{48,40},{56,48},{0,56},{9,1},... | collective-permute-start | bytes 6152 | tf_op jit(solution)/shard_map/ppermute | solution.py:30
  409.5 10.3 %collective-permute-start.77 = (f32[1,2,66,1]{2,3,1,0:T(1,128)}, f32[1,2,66,1]{2,3,1,0:T(1,128)}, u32[]{:S(2)}, u32[]{:S(2)}) collective-permute-start(f32[1,2,66,1]{2,3,1,0:T(1,128)} %get-tuple-element.368), channel_id=1, source_target_pairs={{0,1},{1,2},{2,3},{3,4},{4,5},{5,6},{6,7},{7,0},{8,9},{9,10},{10,1... | collective-permute-start | bytes 1592 | tf_op jit(solution)/shard_map/ppermute | solution.py:27
  409.5 10.3 %collective-permute-start.76 = (f32[1,2,66,1]{2,3,1,0:T(1,128)}, f32[1,2,66,1]{2,3,1,0:T(1,128)}, u32[]{:S(2)}, u32[]{:S(2)}) collective-permute-start(f32[1,2,66,1]{2,3,1,0:T(1,128)} %get-tuple-element.367), channel_id=1, source_target_pairs={{1,0},{2,1},{3,2},{4,3},{5,4},{6,5},{7,6},{0,7},{9,8},{10,9},{11,1... | collective-permute-start | bytes 1592 | tf_op jit(solution)/shard_map/ppermute | solution.py:30
  421.2 5.1 collective-permute-start.78
  441.9 6.8 collective-permute-start.84
  464.5 11.8 %collective-permute-start.91 = (f32[1,2,1,256]{2,3,1,0:T(8,128)S(1)}, f32[1,2,1,256]{2,3,1,0:T(8,128)S(1)}, u32[]{:S(2)}, u32[]{:S(2)}) collective-permute-start(f32[1,2,1,256]{2,3,1,0:T(8,128)S(1)} %get-tuple-element.401), channel_id=1, source_target_pairs={{8,0},{16,8},{24,16},{32,24},{40,32},{48,40},{56,48},{0,56},{9,1},... | collective-permute-start | bytes 6152 | tf_op jit(solution)/shard_map/ppermute | solution.py:30
  470.5 5.8 collective-permute-start.90
  476.9 10.0 %collective-permute-start.93 = (f32[1,2,66,1]{2,3,1,0:T(1,128)}, f32[1,2,66,1]{2,3,1,0:T(1,128)}, u32[]{:S(2)}, u32[]{:S(2)}) collective-permute-start(f32[1,2,66,1]{2,3,1,0:T(1,128)} %get-tuple-element.366), channel_id=1, source_target_pairs={{0,1},{1,2},{2,3},{3,4},{4,5},{5,6},{6,7},{7,0},{8,9},{9,10},{10,1... | collective-permute-start | bytes 1592 | tf_op jit(solution)/shard_map/ppermute | solution.py:27
  476.9 10.0 %collective-permute-start.92 = (f32[1,2,66,1]{2,3,1,0:T(1,128)}, f32[1,2,66,1]{2,3,1,0:T(1,128)}, u32[]{:S(2)}, u32[]{:S(2)}) collective-permute-start(f32[1,2,66,1]{2,3,1,0:T(1,128)} %get-tuple-element.365), channel_id=1, source_target_pairs={{1,0},{2,1},{3,2},{4,3},{5,4},{6,5},{7,6},{0,7},{9,8},{10,9},{11,1... | collective-permute-start | bytes 1592 | tf_op jit(solution)/shard_map/ppermute | solution.py:30
  508.0 6.9 collective-permute-start.100
  532.2 10.6 %collective-permute-start.107 = (f32[1,2,1,256]{2,3,1,0:T(8,128)S(1)}, f32[1,2,1,256]{2,3,1,0:T(8,128)S(1)}, u32[]{:S(2)}, u32[]{:S(2)}) collective-permute-start(f32[1,2,1,256]{2,3,1,0:T(8,128)S(1)} %get-tuple-element.397), channel_id=1, source_target_pairs={{8,0},{16,8},{24,16},{32,24},{40,32},{48,40},{56,48},{0,56},{9,1},... | collective-permute-start | bytes 6152 | tf_op jit(solution)/shard_map/ppermute | solution.py:30
  543.6 10.1 %collective-permute-start.109 = (f32[1,2,66,1]{2,3,1,0:T(1,128)}, f32[1,2,66,1]{2,3,1,0:T(1,128)}, u32[]{:S(2)}, u32[]{:S(2)}) collective-permute-start(f32[1,2,66,1]{2,3,1,0:T(1,128)} %get-tuple-element.364), channel_id=1, source_target_pairs={{0,1},{1,2},{2,3},{3,4},{4,5},{5,6},{6,7},{7,0},{8,9},{9,10},{10,1... | collective-permute-start | bytes 1592 | tf_op jit(solution)/shard_map/ppermute | solution.py:27
  543.7 10.0 %collective-permute-start.108 = (f32[1,2,66,1]{2,3,1,0:T(1,128)}, f32[1,2,66,1]{2,3,1,0:T(1,128)}, u32[]{:S(2)}, u32[]{:S(2)}) collective-permute-start(f32[1,2,66,1]{2,3,1,0:T(1,128)} %get-tuple-element.363), channel_id=1, source_target_pairs={{1,0},{2,1},{3,2},{4,3},{5,4},{6,5},{7,6},{0,7},{9,8},{10,9},{11,1... | collective-permute-start | bytes 1592 | tf_op jit(solution)/shard_map/ppermute | solution.py:30
  575.9 10.0 %collective-permute-start.117 = (f32[1,2,1,256]{2,3,1,0:T(8,128)S(1)}, f32[1,2,1,256]{2,3,1,0:T(8,128)S(1)}, u32[]{:S(2)}, u32[]{:S(2)}) collective-permute-start(f32[1,2,1,256]{2,3,1,0:T(8,128)S(1)} %get-tuple-element.394), channel_id=1, source_target_pairs={{8,0},{16,8},{24,16},{32,24},{40,32},{48,40},{56,48},{0,56},{9,1},... | collective-permute-start | bytes 6152 | tf_op jit(solution)/shard_map/ppermute | solution.py:30
  586.0 5.1 collective-permute-start.119
  613.2 86.6 %all-to-all-start = ((f32[2,4,2,4,64,256]{5,4,3,2,1,0:T(8,128)}), f32[2,4,2,4,64,256]{5,4,3,2,1,0:T(8,128)}, u32[]{:S(2)}, u32[]{:S(2)}) async-start(f32[2,4,2,4,64,256]{5,4,3,2,1,0:T(8,128)} %copy.543), calls=%async_computation | async-start | bytes 8388608 | tf_op jit(solution)/shard_map/all_to_all | solution.py:171
  618.9 43.1 %collective-permute-start.120 = (f32[2,4,64]{1,2,0:T(8,128)S(1)}, f32[2,4,64]{1,2,0:T(8,128)S(1)}, u32[]{:S(2)}, u32[]{:S(2)}) collective-permute-start(f32[2,4,64]{1,2,0:T(8,128)S(1)} %copy-done.41), channel_id=1, source_target_pairs={{0,1},{1,0},{2,3},{3,2},{4,5},{5,4},{6,7},{7,6},{8,9},{9,8},{10,11... | collective-permute-start | bytes 6152 | tf_op jit(solution)/shard_map/ppermute | solution.py:41
  665.7 9.6 %collective-permute-start.122 = (f32[2,4,64]{1,2,0:T(8,128)S(1)}, f32[2,4,64]{1,2,0:T(8,128)S(1)}, u32[]{:S(2)}, u32[]{:S(2)}) collective-permute-start(f32[2,4,64]{1,2,0:T(8,128)S(1)} %add.751), channel_id=1, source_target_pairs={{0,4},{1,5},{2,6},{3,7},{4,0},{5,1},{6,2},{7,3},{8,12},{9,13},{10,... | collective-permute-start | bytes 6152 | tf_op jit(solution)/shard_map/ppermute | solution.py:41
  675.8 8.2 %collective-permute-start.123 = (f32[2]{0:T(128)S(1)}, f32[2]{0:T(128)S(1)}, u32[]{:S(2)}, u32[]{:S(2)}) collective-permute-start(f32[2]{0:T(128)S(1)} %broadcast_multiply_fusion.5), channel_id=1, source_target_pairs={{0,8},{8,0},{16,24},{24,16},{32,40},{40,32},{48,56},{56,48},{1,9},... | collective-permute-start | bytes 32 | tf_op jit(solution)/shard_map/ppermute | solution.py:41
  (130 other events, 1039.0 us)
